TPU v7x, 512 devices: a whole 4x8x8 slice. The times are simulated.
512 devices in a mesh: row: 32 (over y_hi, z), proto: 16 (over x, y_lo, core).
Axes of the slice: x: 4, y: 8 (y_hi: 4, y_lo: 2; y = y_hi * 2 + y_lo), z: 8, core: 2. Of those that a mesh axis runs over, the one named last changes fastest.
Arguments:
- embeddings: bfloat16 [8192, 128], P('row'), may hold values from -6.75 to 6.75
- second_view: bfloat16 [8192, 128], P('row'), may hold values from -6.75 to 6.75
- prototypes: bfloat16 [65536, 128], P('proto'), may hold values from -6.75 to 6.75
- row_scale: float32 [8192], P('row'), may hold values from 1 to 16, as said below
- col_scale: float32 [65536], P('proto'), may hold values from 1 to 16, as said below
Outputs:
- embed_grad: float32 [8192, 128], P(('row', 'proto'))
- proto_grad: float32 [65536, 128], P(('proto', 'row'))
Inputs may be any that keep to these rules, and one draw needn't show every extreme that they name: `row_scale`: positive scalings. `col_scale`: positive scalings.
All inputs are finite; a program needn't handle non-finite values.
Results may differ from a plain program's by a relative error of at most 0.0025.
Values may be sent and summed in bfloat16 or wider, within the bound.
A program may use at most 64 MiB of HBM per device.

v0:
```python
import jax
import jax.numpy as jnp
from jax import lax
from jax.sharding import PartitionSpec as P

ITERS = 4


def contract_rows(left, right):
    return lax.dot_general(
        left, right, (((0,), (0,)), ((), ())), preferred_element_type=jnp.float32
    )


def contract_width(left, right):
    return lax.dot_general(
        left, right, (((1,), (1,)), ((), ())), preferred_element_type=jnp.float32
    )


def per_device(embeddings, second_view, prototypes, row_scale, col_scale):
    feat_width = embeddings.shape[1]
    proto_count = prototypes.shape[0]
    logit_scale = 1.0 / (0.05 * feat_width)
    view_scale = 1.0 / (0.1 * feat_width)
    plan_mass = 64.0 * proto_count * lax.axis_size("proto")

    def make_plan():
        logits = contract_width(embeddings, prototypes) * logit_scale
        return row_scale[:, None] * col_scale[None, :] * jnp.exp(logits) / plan_mass

    def make_cot():
        return -contract_width(second_view, prototypes) * view_scale

    stored_plan = make_plan()
    cotangent = make_cot()
    weighted = stored_plan * cotangent

    def plan_now():
        return make_plan()

    row_mass, row_weight = lax.psum((stored_plan.sum(1), weighted.sum(1)), "proto")
    row_dual = row_weight / row_mass
    col_mass, col_weight = lax.psum((stored_plan.sum(0), weighted.sum(0)), "row")

    def solve_cols(duals_rows):
        product = lax.psum(jnp.dot(duals_rows, plan_now(), precision=lax.Precision.HIGHEST), "row")
        return (col_weight - product) / col_mass

    col_dual = solve_cols(row_dual)
    for sweep in range(ITERS - 1):
        product = lax.psum(jnp.dot(plan_now(), col_dual, precision=lax.Precision.HIGHEST), "proto")
        row_dual = (row_weight - product) / row_mass
        col_dual = solve_cols(row_dual)
    final_plan, final_cot = (make_plan(), make_cot())
    logit_grad = final_plan * (final_cot - row_dual[:, None] - col_dual[None, :])
    scaled_grad = (logit_scale * logit_grad).astype(jnp.bfloat16)
    scaled_plan = (-view_scale * final_plan).astype(jnp.bfloat16)
    embed_grad = lax.psum_scatter(
        jnp.dot(scaled_grad, prototypes, preferred_element_type=jnp.float32),
        "proto",
        scatter_dimension=0,
        tiled=True,
    )
    stacked = jnp.concatenate((scaled_grad, scaled_plan), 0)
    sources = jnp.concatenate((embeddings, second_view), 0)
    proto_grad = lax.psum_scatter(
        contract_rows(stacked, sources), "row", scatter_dimension=0, tiled=True
    )
    return (embed_grad, proto_grad)


def solution(mesh):
    return jax.shard_map(
        per_device,
        mesh=mesh,
        in_specs=(P("row", None), P("row", None), P("proto", None), P("row"), P("proto")),
        out_specs=(P(("row", "proto"), None), P(("proto", "row"), None)),
        check_vma=False,
    )
```

profile of v0, /device:TPU:2, one launch (start us, length us, event | category | flops | bytes accessed | tf_op | source)
XLA Modules:
  0.0 1084.0 jit_solution(11245116675598459363)
XLA Ops:
  7.2 0.0 copy-start
  7.2 0.0 copy-start.2
  7.2 0.0 reduce-scatter.3.cloned.1.call-start
  7.2 1.2 copy-done
  8.4 1.7 fusion.2
  10.1 0.0 copy-done.2
  10.1 0.0 copy-start.1
  10.1 3.3 multiply_reduce_fusion.1
  13.5 0.0 copy-done.1
  13.5 25.7 %all-reduce.1 = (f32[256]{0:T(256)S(1)}, f32[256]{0:T(256)S(1)}) all-reduce(f32[256]{0:T(256)S(1)} %get-tuple-element.2, f32[256]{0:T(256)S(1)} %get-tuple-element.4), channel_id=1, replica_groups=mesh['row'=32,'proto'=16] {'proto'}, use_global_device_ids=true, to_apply=%region_1.0 | all-reduce | flops 512 | bytes 4096 | tf_op jit(solution)/shard_map/psum | solution.py:42
  39.2 4.3 fusion.14
  43.5 161.7 %all-reduce = (f32[4096]{0:T(1024)S(1)}, f32[4096]{0:T(1024)S(1)}, f32[4096]{0:T(1024)S(1)}) all-reduce(f32[4096]{0:T(1024)S(1)} %get-tuple-element.5, f32[4096]{0:T(1024)S(1)} %get-tuple-element.3, f32[4096]{0:T(1024)S(1)} %bitcast.27), channel_id=1, replica_groups=mesh['row'=32,'proto'=16] {'row'}, use_global_device_ids=true, to_apply=%region_8.0 | all-reduce | flops 12288 | bytes 98304 | tf_op jit(solution)/shard_map/psum | solution.py:44
  205.3 5.5 fusion.12
  210.8 27.1 %psum.82 = f32[256]{0:T(256)S(1)} all-reduce(f32[256]{0:T(256)S(1)} %bitcast.36), channel_id=1, replica_groups=mesh['row'=32,'proto'=16] {'proto'}, use_global_device_ids=true, to_apply=%region_9.0 | all-reduce | flops 256 | bytes 2048 | tf_op jit(solution)/shard_map/psum | solution.py:52
  238.0 4.3 fusion.11
  242.3 152.3 %psum.83 = f32[4096]{0:T(1024)S(1)} all-reduce(f32[4096]{0:T(1024)S(1)} %bitcast.28), channel_id=1, replica_groups=mesh['row'=32,'proto'=16] {'row'}, use_global_device_ids=true, to_apply=%region_10.0 | all-reduce | flops 4096 | bytes 32768 | tf_op jit(solution)/shard_map/psum | solution.py:47
  394.6 5.5 fusion.10
  400.1 27.1 %psum.84 = f32[256]{0:T(256)S(1)} all-reduce(f32[256]{0:T(256)S(1)} %bitcast.37), channel_id=1, replica_groups=mesh['row'=32,'proto'=16] {'proto'}, use_global_device_ids=true, to_apply=%region_11.0 | all-reduce | flops 256 | bytes 2048 | tf_op jit(solution)/shard_map/psum | solution.py:52
  427.3 4.3 fusion.9
  431.6 152.1 %psum.85 = f32[4096]{0:T(1024)S(1)} all-reduce(f32[4096]{0:T(1024)S(1)} %bitcast.29), channel_id=1, replica_groups=mesh['row'=32,'proto'=16] {'row'}, use_global_device_ids=true, to_apply=%region_12.0 | all-reduce | flops 4096 | bytes 32768 | tf_op jit(solution)/shard_map/psum | solution.py:47
  583.8 5.5 fusion.8
  589.3 27.1 %psum.86 = f32[256]{0:T(256)S(1)} all-reduce(f32[256]{0:T(256)S(1)} %bitcast.38), channel_id=1, replica_groups=mesh['row'=32,'proto'=16] {'proto'}, use_global_device_ids=true, to_apply=%region_13.0 | all-reduce | flops 256 | bytes 2048 | tf_op jit(solution)/shard_map/psum | solution.py:52
  616.4 4.3 fusion.7
  620.8 152.3 %psum.87 = f32[4096]{0:T(1024)S(1)} all-reduce(f32[4096]{0:T(1024)S(1)} %bitcast.30), channel_id=1, replica_groups=mesh['row'=32,'proto'=16] {'row'}, use_global_device_ids=true, to_apply=%region_14.0 | all-reduce | flops 4096 | bytes 32768 | tf_op jit(solution)/shard_map/psum | solution.py:47
  773.1 0.0 copy-start.3
  773.1 6.1 multiply_convert_fusion
  779.3 1.4 fusion.27
  780.6 0.0 reduce-scatter.3.cloned.1.call-update
  780.6 0.0 reduce-scatter.5.cloned.1.call-start
  780.7 0.0 copy-done.3
  780.7 4.2 fusion.3
  784.9 0.0 reduce-scatter.5.cloned.1.call-update
  784.9 53.0 %reduce-scatter.3.cloned.1.call-done = f32[16,128]{1,0:T(8,128)} async-done(((f32[256,128]{1,0:T(8,128)}), f32[16,128]{1,0:T(8,128)}) %reduce-scatter.3.cloned.1.call-update) | async-done | bytes 8208 | tf_op jit(solution)/shard_map/reduce_scatter | solution.py:59
  837.9 239.3 %reduce-scatter.5.cloned.1.call-done = f32[128,128]{1,0:T(8,128)} async-done(((f32[4096,128]{1,0:T(8,128)}), f32[128,128]{1,0:T(8,128)}) %reduce-scatter.5.cloned.1.call-update) | async-done | bytes 65552 | tf_op jit(solution)/shard_map/reduce_scatter | solution.py:67
  (8 shorter events, 0.1 us)
Async XLA Ops:
  7.2 1.2 copy-start
  7.2 3.0 copy-start.2
  7.2 830.8 %reduce-scatter.3.cloned.1.call-start = ((), (), s32[]{:S(2)}) async-start(), calls=%async_computation.2 | async-start | bytes 139264 | tf_op jit(solution)/shard_map/reduce_scatter | solution.py:59
  10.1 3.3 copy-start.1
  773.1 7.6 copy-start.3
  780.6 296.6 %reduce-scatter.5.cloned.1.call-start = ((), (), s32[]{:S(2)}) async-start(), calls=%async_computation.3 | async-start | bytes 2162688 | tf_op jit(solution)/shard_map/reduce_scatter | solution.py:67
Sparse Core Ops, SparseCore 0:
  780.8 57.1 reduce-scatter.2
  842.9 234.2 reduce-scatter.4
where the time goes:
time: 1080 us
  blocking collectives  726 us (67%)
  waiting for transfers between devices  292 us (27%)
  matrix products  44.6 us (4%)
  between operations  14.1 us (1%)
    psum x3, blocking collectives, solve_cols(): lax.psum(jnp.dot(duals_rows, plan_now(), precision=lax.Precision.HIGHEST)...  457 us
    reduce_scatter x1, waiting for transfers between devices, per_device(): lax.psum_scatter(contract_rows(stacked, sources), 'row', scatter_dimensio...  239 us
    psum x1, blocking collectives, per_device(): lax.psum((stored_plan.sum(0), weighted.sum(0)), 'row')  162 us
    psum x3, blocking collectives, per_device(): lax.psum(jnp.dot(plan_now(), col_dual, precision=lax.Precision.HIGHEST),...  81.4 us
    reduce_scatter x1, waiting for transfers between devices, per_device(): lax.psum_scatter(jnp.dot(scaled_grad, prototypes, preferred_element_type=...  53 us
    psum x1, blocking collectives, per_device(): lax.psum((stored_plan.sum(1), weighted.sum(1)), 'proto')  25.7 us
  transfers between devices with their start and end apart: 2, of which 2 were waited for; matrix products, arithmetic and copies ran while one was open for 0% of the time, Pallas kernels for 0%

commit v1 on v0

--- a/solution.py
+++ b/solution.py
@@ -44,7 +44,14 @@
     col_mass, col_weight = lax.psum((stored_plan.sum(0), weighted.sum(0)), "row")
 
     def solve_cols(duals_rows):
-        product = lax.psum(jnp.dot(duals_rows, plan_now(), precision=lax.Precision.HIGHEST), "row")
+
+        def feed_the_case(payload, lane_axis):
+            parts_out = lax.all_gather(payload, axis_name=lane_axis).sum(axis=0)
+            return parts_out
+
+        product = feed_the_case(
+            jnp.dot(duals_rows, plan_now(), precision=lax.Precision.HIGHEST), "row"
+        )
         return (col_weight - product) / col_mass
 
     col_dual = solve_cols(row_dual)

time: 1080 us -> 945 us (0.88)
  blocking collectives: 726 us -> 584 us
    psum x3 -> x0, blocking collectives: 457 us -> none  [solve_cols(): lax.psum(jnp.dot(duals_rows, plan_now(), precision=lax.Precision.HIGHEST)...]
    all_gather x0 -> x4, blocking collectives: none -> 325 us  [feed_the_case(): parts_out = lax.all_gather(payload, axis_name=lane_axis).sum(axis=0)]
where the time goes in v1:
time: 945 us
  blocking collectives  584 us (62%)
  waiting for transfers between devices  294 us (31%)
  matrix products  44.6 us (5%)
  between operations  14.2 us (2%)
    all_gather x4, blocking collectives, feed_the_case(): parts_out = lax.all_gather(payload, axis_name=lane_axis).sum(axis=0)  325 us
    reduce_scatter x1, waiting for transfers between devices, per_device(): lax.psum_scatter(contract_rows(stacked, sources), 'row', scatter_dimensio...  239 us
    psum x1, blocking collectives, per_device(): lax.psum((stored_plan.sum(0), weighted.sum(0)), 'row')  152 us
    psum x3, blocking collectives, per_device(): lax.psum(jnp.dot(plan_now(), col_dual, precision=lax.Precision.HIGHEST),...  81.3 us
    reduce_scatter x1, waiting for transfers between devices, per_device(): lax.psum_scatter(jnp.dot(scaled_grad, prototypes, preferred_element_type=...  54.4 us
    psum x1, blocking collectives, per_device(): lax.psum((stored_plan.sum(1), weighted.sum(1)), 'proto')  25.7 us
  transfers between devices with their start and end apart: 2, of which 2 were waited for; matrix products, arithmetic and copies ran while one was open for 0% of the time, Pallas kernels for 0%

profile of v1, /device:TPU:2, one launch (start us, length us, event | category | flops | bytes accessed | tf_op | source)
XLA Modules:
  0.0 944.5 jit_solution(14442879556594504887)
XLA Ops:
  7.2 0.0 copy-start
  7.2 0.0 copy-start.2
  7.2 0.0 reduce-scatter.3.cloned.1.call-start
  7.2 1.2 copy-done
  8.4 1.7 fusion.2
  10.1 0.0 copy-done.2
  10.1 0.0 copy-start.1
  10.1 3.3 multiply_reduce_fusion.1
  13.5 0.0 copy-done.1
  13.5 25.7 %all-reduce.1 = (f32[256]{0:T(256)S(1)}, f32[256]{0:T(256)S(1)}) all-reduce(f32[256]{0:T(256)S(1)} %get-tuple-element.4, f32[256]{0:T(256)S(1)} %get-tuple-element.2), channel_id=1, replica_groups=mesh['row'=32,'proto'=16] {'proto'}, use_global_device_ids=true, to_apply=%region_5.0 | all-reduce | flops 512 | bytes 4096 | tf_op jit(solution)/shard_map/psum | solution.py:42
  39.2 4.3 fusion.14
  43.5 88.1 %all-gather = f32[131072]{0:T(1024)S(1)} all-gather(f32[4096]{0:T(1024)S(1)} %bitcast.27), channel_id=2, replica_groups=mesh['row'=32,'proto'=16] {'row'}, dimensions={0}, use_global_device_ids=true | all-gather | bytes 540672 | tf_op jit(solution)/shard_map/all_gather | solution.py:49
  131.7 0.1 reshape.8
  131.8 152.1 %all-reduce = (f32[4096]{0:T(1024)S(1)}, f32[4096]{0:T(1024)S(1)}) all-reduce(f32[4096]{0:T(1024)S(1)} %get-tuple-element.5, f32[4096]{0:T(1024)S(1)} %get-tuple-element.3), channel_id=1, replica_groups=mesh['row'=32,'proto'=16] {'row'}, use_global_device_ids=true, to_apply=%region_8.0 | all-reduce | flops 8192 | bytes 65536 | tf_op jit(solution)/shard_map/psum | solution.py:44
  283.9 5.5 fusion.12
  289.4 27.1 %psum.53 = f32[256]{0:T(256)S(1)} all-reduce(f32[256]{0:T(256)S(1)} %bitcast.36), channel_id=1, replica_groups=mesh['row'=32,'proto'=16] {'proto'}, use_global_device_ids=true, to_apply=%region_9.0 | all-reduce | flops 256 | bytes 2048 | tf_op jit(solution)/shard_map/psum | solution.py:59
  316.5 4.3 fusion.11
  320.8 78.3 %all-gather.1 = f32[131072]{0:T(1024)S(1)} all-gather(f32[4096]{0:T(1024)S(1)} %bitcast.28), channel_id=3, replica_groups=mesh['row'=32,'proto'=16] {'row'}, dimensions={0}, use_global_device_ids=true | all-gather | bytes 540672 | tf_op jit(solution)/shard_map/all_gather | solution.py:49
  399.1 0.1 reshape.9
  399.2 0.1 reduce_sum.77
  399.3 5.5 fusion.10
  404.8 27.1 %psum.54 = f32[256]{0:T(256)S(1)} all-reduce(f32[256]{0:T(256)S(1)} %bitcast.37), channel_id=1, replica_groups=mesh['row'=32,'proto'=16] {'proto'}, use_global_device_ids=true, to_apply=%region_11.0 | all-reduce | flops 256 | bytes 2048 | tf_op jit(solution)/shard_map/psum | solution.py:59
  432.0 4.3 fusion.9
  436.3 80.2 %all-gather.2 = f32[131072]{0:T(1024)S(1)} all-gather(f32[4096]{0:T(1024)S(1)} %bitcast.29), channel_id=4, replica_groups=mesh['row'=32,'proto'=16] {'row'}, dimensions={0}, use_global_device_ids=true | all-gather | bytes 540672 | tf_op jit(solution)/shard_map/all_gather | solution.py:49
  516.5 0.1 reshape.10
  516.6 0.1 reduce_sum.78
  516.7 5.5 fusion.8
  522.2 27.1 %psum.55 = f32[256]{0:T(256)S(1)} all-reduce(f32[256]{0:T(256)S(1)} %bitcast.38), channel_id=1, replica_groups=mesh['row'=32,'proto'=16] {'proto'}, use_global_device_ids=true, to_apply=%region_13.0 | all-reduce | flops 256 | bytes 2048 | tf_op jit(solution)/shard_map/psum | solution.py:59
  549.4 4.3 fusion.7
  553.7 78.4 %all-gather.3 = f32[131072]{0:T(1024)S(1)} all-gather(f32[4096]{0:T(1024)S(1)} %bitcast.30), channel_id=5, replica_groups=mesh['row'=32,'proto'=16] {'row'}, dimensions={0}, use_global_device_ids=true | all-gather | bytes 540672 | tf_op jit(solution)/shard_map/all_gather | solution.py:49
  632.2 0.1 reshape.11
  632.3 0.1 reduce_sum.79
  632.4 0.0 copy-start.3
  632.4 6.1 multiply_convert_fusion
  638.5 1.3 fusion.27
  639.9 0.0 reduce-scatter.3.cloned.1.call-update
  639.9 0.0 reduce-scatter.5.cloned.1.call-start
  639.9 0.0 copy-done.3
  639.9 4.2 fusion.3
  644.2 0.0 reduce-scatter.5.cloned.1.call-update
  644.2 54.4 %reduce-scatter.3.cloned.1.call-done = f32[16,128]{1,0:T(8,128)} async-done(((f32[256,128]{1,0:T(8,128)}), f32[16,128]{1,0:T(8,128)}) %reduce-scatter.3.cloned.1.call-update) | async-done | bytes 8208 | tf_op jit(solution)/shard_map/reduce_scatter | solution.py:66
  698.7 239.0 %reduce-scatter.5.cloned.1.call-done = f32[128,128]{1,0:T(8,128)} async-done(((f32[4096,128]{1,0:T(8,128)}), f32[128,128]{1,0:T(8,128)}) %reduce-scatter.5.cloned.1.call-update) | async-done | bytes 65552 | tf_op jit(solution)/shard_map/reduce_scatter | solution.py:74
  (9 shorter events, 0.1 us)
Async XLA Ops:
  7.2 1.2 copy-start
  7.2 3.0 copy-start.2
  7.2 691.5 %reduce-scatter.3.cloned.1.call-start = ((), (), s32[]{:S(2)}) async-start(), calls=%async_computation.2 | async-start | bytes 139264 | tf_op jit(solution)/shard_map/reduce_scatter | solution.py:66
  10.1 3.3 copy-start.1
  632.4 7.6 copy-start.3
  639.9 297.8 %reduce-scatter.5.cloned.1.call-start = ((), (), s32[]{:S(2)}) async-start(), calls=%async_computation.3 | async-start | bytes 2162688 | tf_op jit(solution)/shard_map/reduce_scatter | solution.py:74
Sparse Core Ops, SparseCore 0:
  640.0 58.6 reduce-scatter.2
  703.6 233.9 reduce-scatter.4
